TPU v7x, 32 devices: a whole 2x2x4 slice. The times are simulated.
32 devices in a mesh: kpool: 8 (over y, x, core), band: 4 (over z).
Axes of the slice: x: 2, y: 2, z: 4, core: 2. Of those that a mesh axis runs over, the one named last changes fastest.
Arguments:
- psi: bfloat16 [8, 2, 4, 48, 2304], P('kpool', None, 'band'), may hold values from -6 to 6
- kpoint_of_pool: int32 [8], replicated, may hold values from 0 to 7, each once
Outputs:
- exchange: float32 [8, 2, 4, 48, 2304], P('kpool', None, 'band')
Inputs may be any that keep to these rules, and one draw needn't show every extreme that they name: `kpoint_of_pool`: each value appears once.
All inputs are finite; a program needn't handle non-finite values.
Results may differ from a plain program's by a relative error of at most 0.0003.
Values may be sent and summed in bfloat16 or wider, within the bound.
A program may use at most 64 MiB of HBM per device.

v0:
```python
import functools
import math

import jax
import jax.numpy as jnp
import numpy as np
from jax import lax
from jax.experimental import pallas as pl
from jax.experimental.pallas import tpu as pltpu
from jax.sharding import PartitionSpec as P

KMESH = 4
ROUNDS = 1
LANES = 128
HALF = 64
PITCH = 8
MESH = pl.DeviceIdType.MESH


def kpoint_coords(labels):
    first = labels % KMESH
    second = labels // KMESH % KMESH
    third = labels // (KMESH * KMESH)
    return jnp.stack([first, second, third], axis=1).astype(jnp.float32) / KMESH


def two_parts(table):
    high = table.astype(jnp.bfloat16)
    low = (table - high.astype(np.float32)).astype(jnp.bfloat16)
    return high, low


def dft_tables(grid):
    index = np.arange(grid)
    angles = (index[:, None] * index[None, :] % grid) * (2.0 * math.pi / grid)
    cosine = np.cos(angles).astype(np.float32)
    sine = np.sin(angles).astype(np.float32)
    lanes = []
    for sign in (1.0, -1.0):
        full = np.zeros((LANES, LANES), np.float32)
        full[:grid, :grid] = cosine
        full[HALF : HALF + grid, HALF : HALF + grid] = cosine
        full[:grid, HALF : HALF + grid] = -sign * sine
        full[HALF : HALF + grid, :grid] = sign * sine
        high, low = two_parts(full)
        lanes.append(np.block([[high, low], [high, np.zeros_like(low)]]))
    high, low = two_parts(np.concatenate([cosine, sine], axis=0))
    rows = np.concatenate([high, high, low], axis=1)
    return np.stack(lanes), rows


def split(x):
    high = x.astype(jnp.bfloat16)
    low = (x - high.astype(jnp.float32)).astype(jnp.bfloat16)
    return high, low


def visits(ring, n):
    return [n] + sorted((m for m in range(ring) if m != n), key=lambda m: (abs(m - n), (m - n) % 2 * 0 + (m ^ 1 != n)))


def squares(offset, grid, axis_len):
    index = jnp.arange(axis_len, dtype=jnp.int32) % (HALF if axis_len > grid else grid)
    freq = jnp.where(index < grid // 2, index, index - grid).astype(jnp.float32)
    cut = (index == grid // 2) | (index >= grid)
    return jnp.where(cut, 1e30, (offset + freq) ** 2)


def kernel(grid, ring, pools, pitch, sent_ref, a1_ref, a2_ref, ax_ref, ay_ref, az_ref, lanes_ref, rows_ref, out_ref,
           bufs, field, acc1, acc2, v_ref, recv_sem, send_sem):
    points = grid * grid
    packed = sent_ref.shape[0]
    quarter = points - packed
    me, n = lax.axis_index("kpool"), lax.axis_index("band")
    odd = me % 2
    turn = 1 - 2 * odd
    near = (me + turn + pools) % pools
    far = (me - turn + pools) % pools
    beyond = (me + 2 * turn + pools) % pools
    before = (me - 2 * turn + pools) % pools

    barrier = pltpu.get_barrier_semaphore()

    def hail(pool, band):
        pl.semaphore_signal(barrier, inc=1, device_id=(pool, band), device_id_type=MESH)

    for pool in (near, far, beyond, before):
        hail(pool, n)
    for plane in range(ring):
        @pl.when(n == plane)
        def _():
            count = 4
            for other in (plane - 1, plane + 1):
                if 0 <= other < ring:
                    hail(near, other)
                    hail(me, other)
                    count += 2
            pl.semaphore_wait(barrier, count)

    def place(plane, band, outer):
        return 2 * visits(ring, plane).index(band) + outer

    def copy(source, step, pool, band, slot):
        return pltpu.make_async_remote_copy(
            src_ref=source,
            dst_ref=bufs.at[step, pl.ds(0, packed)],
            send_sem=send_sem.at[slot],
            recv_sem=recv_sem.at[step],
            device_id=(pool, band),
            device_id_type=MESH,
        )

    def sends(plane):
        first = [(sent_ref, place(plane, plane, 0), near, plane, 0)]
        first.append((sent_ref, place(plane, plane, 1), far, plane, 1))
        slot = 2
        for other in (plane - 1, plane + 1):
            if 0 <= other < ring:
                first.append((sent_ref, place(other, plane, 0), near, other, slot))
                slot += 1
        later = {}
        for band in visits(ring, plane)[1:]:
            step = place(plane, band, 0)
            source = bufs.at[step, pl.ds(0, packed)]
            onward = plane + 1 if band < plane else plane - 1
            copies = []
            if 0 <= onward < ring:
                copies.append((source, place(onward, band, 0), me, onward, slot))
                slot += 1
            copies.append((source, place(plane, band, 1), beyond, plane, slot))
            slot += 1
            later[step] = copies
        return first, later

    def arrival(step):
        spot = bufs.at[step, pl.ds(0, packed)]
        pltpu.make_async_copy(spot, spot, recv_sem.at[step]).wait()

    def service(step, moment):
        for plane in range(ring):
            order = visits(ring, plane)
            due = []
            for at, band in enumerate(order):
                if at == 0:
                    continue
                when = 1 if abs(band - plane) == 1 else 2 * at - 1
                due.append((when, 2 * at))

            @pl.when(n == plane)
            def _():
                for when, number in due:
                    @pl.when(moment == when)
                    def _():
                        arrival(number)
                        for c in sends(plane)[1][number]:
                            copy(*c).start()

    for plane in range(ring):
        @pl.when(n == plane)
        def _():
            for c in sends(plane)[0]:
                copy(*c).start()

    lane = lax.broadcasted_iota(jnp.int32, (1, LANES), 1)
    sign = jnp.where(lane < HALF, 1.0, -1.0).astype(jnp.float32)
    scale = grid**1.5 / 16.0 / (grid * grid * grid)

    def make_v(y, carry):
        for which in range(2):
            total = ax_ref[which] + ay_ref[which, pl.ds(y, 1), :] + az_ref[which, 0:1, :]
            v_ref[which, y] = jnp.where(total > 1e29, 0.0, scale / total)
        return carry

    lax.fori_loop(0, grid, make_v, 0)

    def swap(x):
        return pltpu.roll(x, HALF, 1)

    def turned(x):
        return swap(x) * sign

    def along_lanes(x, which):
        high, low = split(x)
        out = jnp.dot(
            jnp.concatenate([high, low], axis=1), lanes_ref[which], preferred_element_type=jnp.float32
        )
        return out[:, :LANES] + out[:, LANES:]

    def along_rows(xs, sense):
        parts = []
        for x in xs:
            high, low = split(x)
            parts.append(jnp.concatenate([high, low, high], axis=0))
        outs = []
        for at in range(0, len(parts), 2):
            pair = jnp.concatenate(parts[at : at + 2], axis=1)
            out = jnp.dot(rows_ref[...], pair, preferred_element_type=jnp.float32)
            for j in range(len(parts[at : at + 2])):
                piece = out[:, j * LANES : (j + 1) * LANES]
                q = turned(piece[grid:])
                outs.append(piece[:grid] + q if sense > 0 else piece[:grid] - q)
        return outs

    def one_field(step, carry):
        @pl.when(step % 2 == 1)
        def _():
            service(step, step)

        @pl.when(jnp.logical_or(step == 0, step % 2 == 1))
        def _():
            arrival(step)

        which = step % 2
        spread = lane % HALF // 16

        def unstuff(at, carry):
            rows = 48
            total = jnp.zeros((rows, LANES), jnp.float32)
            for c in range(3):
                x = bufs[step, pl.ds(pl.multiple_of(c * quarter + at * rows, 16), rows), :].astype(jnp.float32)
                total = jnp.where(spread == c, pltpu.roll(x, (c * 16 - 48) % LANES, 1), total)
            bufs[step, pl.ds(pl.multiple_of(packed + at * rows, 16), rows), :] = total.astype(jnp.bfloat16)
            return carry

        lax.fori_loop(0, quarter // 48, unstuff, 0)

        def band_rows(x):
            return bufs[step, x * grid : (x + 1) * grid, :].astype(jnp.float32)

        for base in range(0, grid, 4):
            dens = []
            for x in range(base, base + 4):
                b = band_rows(x)
                span = slice(x * grid, (x + 1) * grid)
                dens.append(b * a1_ref[span, :] + swap(b) * a2_ref[span, :])
            spec = along_lanes(jnp.concatenate(dens, axis=0), 0)
            outs = along_rows([spec[j * grid : (j + 1) * grid] for j in range(4)], 1)
            for j in range(4):
                field[(base + j) * pitch : (base + j) * pitch + grid, :] = outs[j]

        for base in range(0, grid, 4):
            xs = [field[pl.ds(base + j, grid, stride=pitch), :] for j in range(4)]
            spec = along_rows(xs, 1)
            spec = [spec[j] * v_ref[which, base + j] for j in range(4)]
            outs = along_rows(spec, -1)
            for j in range(4):
                field[pl.ds(base + j, grid, stride=pitch), :] = outs[j]

        for base in range(0, grid, 4):
            mids = [field[(base + j) * pitch : (base + j) * pitch + grid, :] for j in range(4)]
            outs = along_rows(mids, -1)
            pot = along_lanes(jnp.concatenate(outs, axis=0), 1)
            for j in range(4):
                x = base + j
                b = band_rows(x)
                span = slice(x * grid, (x + 1) * grid)
                piece = pot[j * grid : (j + 1) * grid]
                acc1[span, :] = acc1[span, :] + b * piece
                acc2[span, :] = acc2[span, :] + b * swap(piece)
        return carry

    acc1[...] = jnp.zeros_like(acc1)
    acc2[...] = jnp.zeros_like(acc2)
    lax.fori_loop(0, 2 * ring, one_field, 0)

    weight = -((2.0 * ROUNDS * ring) ** (-0.5))
    first = lane < HALF

    def finish(x, carry):
        rows = pl.ds(pl.multiple_of(x * grid, 16), grid)
        one = acc1[rows, :]
        two = acc2[rows, :]
        real = one - swap(one)
        imag = two + swap(two)
        out_ref[rows, :] = jnp.where(first, real, imag) * weight
        return carry

    lax.fori_loop(0, grid, finish, 0)

    for plane in range(ring):
        @pl.when(n == plane)
        def _():
            begun, later = sends(plane)
            for c in begun:
                copy(*c).wait_send()
            for copies in later.values():
                for c in copies:
                    copy(*c).wait_send()


def per_device(psi, kpoint_of_pool):
    own = psi[0, :, 0]
    grid = own.shape[1]
    ring = lax.axis_size("band")
    pools = lax.axis_size("kpool")
    me = lax.axis_index("kpool")
    coords = kpoint_coords(kpoint_of_pool)
    turn = 1 - 2 * (me % 2)
    here = lax.dynamic_index_in_dim(coords, me, 0, keepdims=False)
    offsets = jnp.stack(
        [
            here - lax.dynamic_index_in_dim(coords, (me + turn + pools) % pools, 0, keepdims=False),
            here - lax.dynamic_index_in_dim(coords, (me - turn + pools) % pools, 0, keepdims=False),
        ]
    )
    along = jax.vmap(lambda o: squares(o, grid, grid))
    ax = jnp.broadcast_to(along(offsets[:, 0])[:, :, None], (2, grid, LANES))
    ay = jnp.broadcast_to(along(offsets[:, 1])[:, :, None], (2, grid, LANES))
    az = jax.vmap(lambda o: squares(o, grid, LANES))(offsets[:, 2])
    az = jnp.broadcast_to(az[:, None, :], (2, 8, LANES))
    points = grid * grid
    kept = grid * 3 // 4
    parts = own.reshape(2, grid, grid, grid)
    extra = parts[:, kept:].reshape(2, grid - kept, grid, 3, 16)
    extra = jnp.moveaxis(extra, 3, 1).reshape(2, kept, grid, 16)
    stuffed = jnp.concatenate([parts[:, :kept], extra], axis=-1)
    stuffed = jnp.concatenate([stuffed[0], stuffed[1]], axis=-1).reshape(kept * grid, LANES)
    wide = jnp.pad(parts.reshape(2, points, grid), ((0, 0), (0, 0), (0, HALF - grid))).astype(jnp.float32)
    a1 = jnp.concatenate([wide[0], -wide[0]], axis=-1)
    a2 = jnp.concatenate([wide[1], wide[1]], axis=-1)
    lanes, rows = dft_tables(grid)
    whole = pl.BlockSpec(memory_space=pltpu.VMEM)
    args = [stuffed, a1, a2, ax, ay, az, jnp.asarray(lanes), jnp.asarray(rows)]
    pitch = grid + PITCH
    total = pl.pallas_call(
        functools.partial(kernel, grid, ring, pools, pitch),
        in_specs=[whole] * len(args),
        out_specs=whole,
        out_shape=jax.ShapeDtypeStruct((points, LANES), jnp.float32),
        scratch_shapes=[
            pltpu.VMEM((2 * ring, points, LANES), jnp.bfloat16),
            pltpu.VMEM((grid * pitch, LANES), jnp.float32),
            pltpu.VMEM((points, LANES), jnp.float32),
            pltpu.VMEM((points, LANES), jnp.float32),
            pltpu.VMEM((2, grid, grid, LANES), jnp.float32),
            pltpu.SemaphoreType.DMA((2 * ring,)),
            pltpu.SemaphoreType.DMA((4 + 2 * ring,)),
        ],
        compiler_params=pltpu.CompilerParams(collective_id=0, has_side_effects=True),
    )(*args)
    result = jnp.stack([total[:, :grid], total[:, HALF : HALF + grid]])
    return result.reshape(1, 2, 1, grid, points)


def solution(mesh):
    in_specs = (P("kpool", None, "band", None, None), P())
    out_specs = P("kpool", None, "band", None, None)
    return jax.shard_map(per_device, mesh=mesh, in_specs=in_specs, out_specs=out_specs, check_vma=False)
```

profile of v0, /device:TPU:0, one launch (start us, length us, event | category | flops | bytes accessed | tf_op | source)
XLA Modules:
  0.0 99.3 jit_solution(10449498358544643032)
XLA Ops:
  0.0 0.7 fusion.2
  0.7 0.1 dynamic-slice_subtract_fusion.1
  0.8 0.1 pad_maximum_fusion.5
  0.9 0.1 multiply_select_fusion.1
  0.9 0.7 broadcast_in_dim.43.ax_ref
  1.6 0.7 broadcast_in_dim.44.ay_ref
  2.3 0.1 multiply_select_fusion
  2.4 0.6 broadcast_in_dim.47.az_ref
  3.0 2.6 %reshape_reshape_squeeze.3 = bf16[2,2304,48]{2,1,0:T(8,128)(2,1)S(1)} reshape(bf16[1,2,1,48,2304]{4,3,2,1,0:T(8,128)(2,1)} %param.4) | data formatting | bytes 884736 | tf_op jit(solution)/shard_map/reshape;reshape;squeeze | solution.py:318
  5.7 0.2 pad_convert_fusion
  5.8 0.2 slice_bitcast_fusion
  6.0 0.1 fusion.8
  6.1 0.0 copy-start
  6.1 2.1 %pad_maximum_fusion = (f32[2304,128]{1,0:T(8,128)}, f32[2304,128]{1,0:T(8,128)}) fusion(f32[2304,64]{1,0:T(8,128)S(1)} %fusion.8, f32[2304,64]{1,0:T(8,128)S(1)} %get-tuple-element.6, f32[2304,64]{1,0:T(8,128)S(1)} %get-tuple-element.5), kind=kLoop, calls=%fused_computation.2 | loop fusion | flops 589824 | bytes 4128768 | tf_op jit(solution)/shard_map/concatenate | solution.py:319
  8.2 0.0 copy-done
  8.2 1.6 %reshape_squeeze.3 = bf16[2,48,48,48]{3,2,1,0:T(8,128)(2,1)S(1)} reshape(bf16[1,2,1,48,2304]{4,3,2,1,0:T(8,128)(2,1)S(1)} %copy-done) | data formatting | bytes 884736 | tf_op jit(solution)/shard_map/reshape;squeeze | solution.py:313
  9.8 0.2 copy.8
  10.1 0.4 copy.10
  10.5 0.1 slice.52
  10.5 0.5 fusion
  11.0 1.0 %pad_maximum_fusion.4.sent_ref = bf16[1728,128]{1,0:T(8,128)(2,1)} fusion(bf16[1728,64]{1,0:T(8,128)(2,1)S(1)} %bitcast.29, bf16[1728,64]{1,0:T(8,128)(2,1)S(1)} %bitcast.28), kind=kLoop, calls=%fused_computation.10 | loop fusion | flops 884736 | bytes 884736 | tf_op jit(solution)/shard_map/concatenate | solution.py:317
  12.0 83.3 %shard_map.46 = f32[2304,128]{1,0:T(8,128)} custom-call(bf16[1728,128]{1,0:T(8,128)(2,1)} %pad_maximum_fusion.4.sent_ref, f32[2304,128]{1,0:T(8,128)} %get-tuple-element.21.a1_ref, f32[2304,128]{1,0:T(8,128)} %get-tuple-element.22.a2_ref, f32[2,48,128]{2,1,0:T(8,128)} %broadcast_in_dim.43.ax_ref, f32[2,48,128]{2,1,0:T(8,128)} %broadcast_in_dim.44.ay_ref, ...), custom_call_target="tpu_custom_call" | custom-call | tf_op jit(solution)/shard_map/pallas_call | solution.py:325
  95.3 2.0 %fusion.9 = (f32[2304,48]{1,0:T(8,128)S(1)}, f32[2304,48]{1,0:T(8,128)S(1)}) fusion(f32[2304,128]{1,0:T(8,128)} %shard_map.46), kind=kLoop, calls=%fused_computation.46 | loop fusion | bytes 1769472 | tf_op jit(solution)/shard_map/slice | solution.py:341
  97.3 0.5 stack.31
  97.8 0.5 stack.32
  98.3 1.0 pad_maximum_fusion.2
  (8 shorter events, 0.1 us)
Async XLA Ops:
  6.1 2.1 %copy-start = (bf16[1,2,1,48,2304]{4,3,2,1,0:T(8,128)(2,1)S(1)}, bf16[1,2,1,48,2304]{4,3,2,1,0:T(8,128)(2,1)}, u32[]{:S(2)}) copy-start(bf16[1,2,1,48,2304]{4,3,2,1,0:T(8,128)(2,1)} %param.4) | copy-start | bytes 1327108
where the time goes:
time: 99.5 us; the launch traced here: 99.3 us
  Pallas kernels  83.3 us (84%)
  local copies, waits for them, and re-layouts  10.1 us (10%)
  other arithmetic  5.81 us (6%)
    pallas_call x1, Pallas kernels, per_device(): pl.pallas_call(functools.partial(kernel, grid, ring, pools, pitch), in_sp...  83.3 us
    another operation x1, local copies, waits for them, and re-layouts, per_device(): parts.reshape(2, points, grid)  2.65 us
    concatenate x1, other arithmetic, per_device(): a1 = jnp.concatenate([wide[0], -wide[0]], axis=-1)  2.1 us
    slice x1, local copies, waits for them, and re-layouts, per_device(): result = jnp.stack([total[:, :grid], total[:, HALF:HALF + grid]])  2 us

commit v1 on v0

v1 whole, which is shorter than its diff:
```python
import functools
import math

import jax
import jax.numpy as jnp
import numpy as np
from jax import lax
from jax.experimental import pallas as pl
from jax.experimental.pallas import tpu as pltpu
from jax.sharding import PartitionSpec as P

KMESH = 4
ROUNDS = 1
LANES = 128
HALF = 64
PITCH = 8
FAR = 1e30
BATCH = 48
MESH = pl.DeviceIdType.MESH


def kpoint_coords(label):
    digits = (label % KMESH, label // KMESH % KMESH, label // (KMESH * KMESH))
    return [digit.astype(jnp.float32) / KMESH for digit in digits]


def two_parts(table):
    high = table.astype(jnp.bfloat16)
    low = (table - high.astype(np.float32)).astype(jnp.bfloat16)
    return high, low


def dft_tables(grid):
    index = np.arange(grid)
    angles = (index[:, None] * index[None, :] % grid) * (2.0 * math.pi / grid)
    cosine = np.cos(angles).astype(np.float32)
    sine = np.sin(angles).astype(np.float32)
    lanes = []
    for sign in (1.0, -1.0):
        full = np.zeros((LANES, LANES), np.float32)
        full[:grid, :grid] = cosine
        full[HALF : HALF + grid, HALF : HALF + grid] = cosine
        full[:grid, HALF : HALF + grid] = -sign * sine
        full[HALF : HALF + grid, :grid] = sign * sine
        high, low = two_parts(full)
        lanes.append(np.block([[high, low], [high, np.zeros_like(low)]]))
    high, low = two_parts(np.concatenate([cosine, sine], axis=0))
    rows = np.concatenate([high, high, low], axis=1)
    return np.stack(lanes), rows


def split(x):
    high = x.astype(jnp.bfloat16)
    low = (x - high.astype(jnp.float32)).astype(jnp.bfloat16)
    return high, low


def visits(ring, n):
    return [n] + sorted((m for m in range(ring) if m != n), key=lambda m: (abs(m - n), (m - n) % 2 * 0 + (m ^ 1 != n)))


def squares(offset, grid, index):
    freq = jnp.where(index < grid // 2, index, index - grid).astype(jnp.float32)
    cut = (index == grid // 2) | (index >= grid)
    return jnp.where(cut, FAR, (offset + freq) ** 2)


def kernel(grid, ring, pools, pitch, batch, label_ref, sent_ref, lanes_ref, rows_ref, out_ref,
           bufs, field, band, a1_ref, a2_ref, acc1, acc2, v_ref, recv_sem, send_sem):
    me, n = lax.axis_index("kpool"), lax.axis_index("band")
    odd = me % 2
    turn = 1 - 2 * odd
    near = (me + turn + pools) % pools
    far = (me - turn + pools) % pools
    beyond = (me + 2 * turn + pools) % pools
    before = (me - 2 * turn + pools) % pools

    barrier = pltpu.get_barrier_semaphore()

    def hail(pool, band):
        pl.semaphore_signal(barrier, inc=1, device_id=(pool, band), device_id_type=MESH)

    for pool in (near, far, beyond, before):
        hail(pool, n)
    for plane in range(ring):
        @pl.when(n == plane)
        def _():
            count = 4
            for other in (plane - 1, plane + 1):
                if 0 <= other < ring:
                    hail(near, other)
                    hail(me, other)
                    count += 2
            pl.semaphore_wait(barrier, count)

    def place(plane, band, outer):
        return 2 * visits(ring, plane).index(band) + outer

    def copy(source, step, pool, band, slot):
        return pltpu.make_async_remote_copy(
            src_ref=source,
            dst_ref=bufs.at[step],
            send_sem=send_sem.at[slot],
            recv_sem=recv_sem.at[step],
            device_id=(pool, band),
            device_id_type=MESH,
        )

    def sends(plane):
        first = [(sent_ref, place(plane, plane, 0), near, plane, 0)]
        first.append((sent_ref, place(plane, plane, 1), far, plane, 1))
        slot = 2
        for other in (plane - 1, plane + 1):
            if 0 <= other < ring:
                first.append((sent_ref, place(other, plane, 0), near, other, slot))
                slot += 1
        later = {}
        for band in visits(ring, plane)[1:]:
            step = place(plane, band, 0)
            source = bufs.at[step]
            onward = plane + 1 if band < plane else plane - 1
            copies = []
            if 0 <= onward < ring:
                copies.append((source, place(onward, band, 0), me, onward, slot))
                slot += 1
            copies.append((source, place(plane, band, 1), beyond, plane, slot))
            slot += 1
            later[step] = copies
        return first, later

    def arrival(step):
        spot = bufs.at[step]
        pltpu.make_async_copy(spot, spot, recv_sem.at[step]).wait()

    def service(step, moment):
        for plane in range(ring):
            order = visits(ring, plane)
            due = []
            for at, band in enumerate(order):
                if at == 0:
                    continue
                when = 1 if abs(band - plane) == 1 else 2 * at - 1
                due.append((when, 2 * at))

            @pl.when(n == plane)
            def _():
                for when, number in due:
                    @pl.when(moment == when)
                    def _():
                        arrival(number)
                        for c in sends(plane)[1][number]:
                            copy(*c).start()

    for plane in range(ring):
        @pl.when(n == plane)
        def _():
            for c in sends(plane)[0]:
                copy(*c).start()

    lane = lax.broadcasted_iota(jnp.int32, (1, LANES), 1)
    sign = jnp.where(lane < HALF, 1.0, -1.0).astype(jnp.float32)
    scale = grid**1.5 / 16.0 / (grid * grid * grid)

    first = lane < HALF
    here = kpoint_coords(label_ref[me])
    column = lax.broadcasted_iota(jnp.int32, (grid, LANES), 0)
    for which, partner in enumerate((near, far)):
        there = kpoint_coords(label_ref[partner])
        off = [here[d] - there[d] for d in range(3)]
        plane_sum = squares(off[1], grid, column) + squares(off[2], grid, lane % HALF)

        def make_v(x, carry):
            shifted = (x - grid * (x // (grid // 2))).astype(jnp.float32) + off[0]
            edge = (x == grid // 2).astype(jnp.float32)
            total = plane_sum + (shifted * shifted + edge * FAR)
            v_ref[which, x] = jnp.where(total > 0.5 * FAR, 0.0, scale / total)
            return carry

        lax.fori_loop(0, grid, make_v, 0)

    def swap(x):
        return pltpu.roll(x, HALF, 1)

    def turned(x):
        return swap(x) * sign

    def tile(source, start):
        at, off = start // LANES, start % LANES
        halves = []
        for part in range(2):
            turn_by = (part * HALF - off) % LANES

            def lanes_of(column):
                x = source[part, :, column * LANES : (column + 1) * LANES].astype(jnp.float32)
                return pltpu.roll(x, turn_by, 1) if turn_by else x

            half = lanes_of(at)
            if off + grid > LANES:
                half = jnp.where(lane < part * HALF + LANES - off, half, lanes_of(at + 1))
            halves.append(half)
        return jnp.where(first, halves[0], halves[1])

    def along_lanes(x, which):
        high, low = split(x)
        out = jnp.dot(
            jnp.concatenate([high, low], axis=1), lanes_ref[which], preferred_element_type=jnp.float32
        )
        return out[:, :LANES] + out[:, LANES:]

    def along_rows(xs, sense):
        parts = []
        for x in xs:
            high, low = split(x)
            parts.append(jnp.concatenate([high, low, high], axis=0))
        outs = []
        for at in range(0, len(parts), 2):
            pair = jnp.concatenate(parts[at : at + 2], axis=1)
            out = jnp.dot(rows_ref[...], pair, preferred_element_type=jnp.float32)
            for j in range(len(parts[at : at + 2])):
                piece = out[:, j * LANES : (j + 1) * LANES]
                q = turned(piece[grid:])
                outs.append(piece[:grid] + q if sense > 0 else piece[:grid] - q)
        return outs

    def one_field(step, carry):
        @pl.when(step % 2 == 1)
        def _():
            service(step, step)

        @pl.when(jnp.logical_or(step == 0, step % 2 == 1))
        def _():
            arrival(step)

        which = step % 2
        source = bufs.at[step]

        for base in range(0, grid, batch):
            dens = []
            for y in range(base, base + batch):
                span = slice(y * grid, (y + 1) * grid)
                b = tile(source, y * grid)
                band[span, :] = b
                dens.append(b * a1_ref[span, :] + swap(b) * a2_ref[span, :])
            spec = along_lanes(jnp.concatenate(dens, axis=0), 0)
            outs = along_rows([spec[j * grid : (j + 1) * grid] for j in range(batch)], 1)
            for j in range(batch):
                field[(base + j) * pitch : (base + j) * pitch + grid, :] = outs[j]

        for base in range(0, grid, batch):
            xs = [field[pl.ds(base + j, grid, stride=pitch), :] for j in range(batch)]
            spec = along_rows(xs, 1)
            spec = [spec[j] * v_ref[which, base + j] for j in range(batch)]
            outs = along_rows(spec, -1)
            for j in range(batch):
                field[pl.ds(base + j, grid, stride=pitch), :] = outs[j]

        for base in range(0, grid, batch):
            mids = [field[(base + j) * pitch : (base + j) * pitch + grid, :] for j in range(batch)]
            outs = along_rows(mids, -1)
            pot = along_lanes(jnp.concatenate(outs, axis=0), 1)
            for j in range(batch):
                y = base + j
                span = slice(y * grid, (y + 1) * grid)
                b = band[span, :]
                piece = pot[j * grid : (j + 1) * grid]
                acc1[span, :] = acc1[span, :] + b * piece
                acc2[span, :] = acc2[span, :] + b * swap(piece)
        return carry

    group = math.lcm(grid, LANES)
    lines = group // grid

    def prepare(g, carry):
        view = sent_ref.at[:, :, pl.ds(pl.multiple_of(g * group, LANES), group)]
        for j in range(lines):
            a = tile(view, j * grid)
            other = swap(a)
            rows = pl.ds(pl.multiple_of((g * lines + j) * grid, 8), grid)
            a1_ref[rows, :] = jnp.where(first, a, -other)
            a2_ref[rows, :] = jnp.where(first, other, a)
        return carry

    lax.fori_loop(0, grid // lines, prepare, 0)
    acc1[...] = jnp.zeros_like(acc1)
    acc2[...] = jnp.zeros_like(acc2)
    lax.fori_loop(0, 2 * ring, one_field, 0)

    weight = -((2.0 * ROUNDS * ring) ** (-0.5))

    def finish(g, carry):
        made = [[None] * (group // LANES) for _ in range(2)]
        for j in range(lines):
            rows = pl.ds(pl.multiple_of((g * lines + j) * grid, 8), grid)
            one = acc1[rows, :]
            two = acc2[rows, :]
            start = j * grid
            at, off = start // LANES, start % LANES
            for part, value in enumerate((one - swap(one), two + swap(two))):
                value = pltpu.roll(value * weight, off, 1) if off else value * weight
                row = made[part]
                row[at] = value if off == 0 else jnp.where(lane < off, row[at], value)
                if off + grid > LANES:
                    row[at + 1] = value
        for part in range(2):
            for at in range(group // LANES):
                lanes_at = pl.ds(pl.multiple_of(g * group + at * LANES, LANES), LANES)
                out_ref[part, :, lanes_at] = made[part][at]
        return carry

    lax.fori_loop(0, grid // lines, finish, 0)

    for plane in range(ring):
        @pl.when(n == plane)
        def _():
            begun, later = sends(plane)
            for c in begun:
                copy(*c).wait_send()
            for copies in later.values():
                for c in copies:
                    copy(*c).wait_send()


def per_device(psi, kpoint_of_pool):
    own = psi[0, :, 0]
    grid, points = own.shape[1], own.shape[2]
    ring = lax.axis_size("band")
    pools = lax.axis_size("kpool")
    lanes, rows = dft_tables(grid)
    whole = pl.BlockSpec(memory_space=pltpu.VMEM)
    pitch = grid + PITCH
    total = pl.pallas_call(
        functools.partial(kernel, grid, ring, pools, pitch, BATCH),
        in_specs=[pl.BlockSpec(memory_space=pltpu.SMEM)] + [whole] * 3,
        out_specs=whole,
        out_shape=jax.ShapeDtypeStruct(own.shape, jnp.float32),
        scratch_shapes=[
            pltpu.VMEM((2 * ring,) + own.shape, jnp.bfloat16),
            pltpu.VMEM((grid * pitch, LANES), jnp.float32),
            pltpu.VMEM((points, LANES), jnp.float32),
            pltpu.VMEM((points, LANES), jnp.float32),
            pltpu.VMEM((points, LANES), jnp.float32),
            pltpu.VMEM((points, LANES), jnp.float32),
            pltpu.VMEM((points, LANES), jnp.float32),
            pltpu.VMEM((2, grid, grid, LANES), jnp.float32),
            pltpu.SemaphoreType.DMA((2 * ring,)),
            pltpu.SemaphoreType.DMA((4 + 2 * ring,)),
        ],
        compiler_params=pltpu.CompilerParams(collective_id=0, has_side_effects=True),
    )(kpoint_of_pool, own, jnp.asarray(lanes), jnp.asarray(rows))
    return total[None, :, None]


def solution(mesh):
    in_specs = (P("kpool", None, "band", None, None), P())
    out_specs = P("kpool", None, "band", None, None)
    return jax.shard_map(per_device, mesh=mesh, in_specs=in_specs, out_specs=out_specs, check_vma=False)
```

time: 99.5 us -> 66.9 us (0.67)
  Pallas kernels: 83.3 us -> 64.6 us
  local copies, waits for them, and re-layouts: 10.1 us -> 2.14 us
  other arithmetic: 5.81 us -> 0 us
    pallas_call x1, Pallas kernels: 83.3 us -> 64.6 us  [per_device(): pl.pallas_call(functools.partial(kernel, grid, ring, pools, pitch, BATCH)...]
    another operation x4 -> x0, local copies, waits for them, and re-layouts: 5.27 us -> none  [the longest x1 2.65 us: per_device(): parts.reshape(2, points, grid)]
    concatenate x3 -> x0, other arithmetic: 3.59 us -> none  [the longest x1 2.1 us: per_device(): a1 = jnp.concatenate([wide[0], -wide[0]], axis=-1)]
    slice x4 -> x0, local copies, waits for them, and re-layouts: 2.26 us -> none  [the longest x1 2 us: per_device(): result = jnp.stack([total[:, :grid], total[:, HALF:HALF + grid]])]
    unnamed x2 -> x1, local copies, waits for them, and re-layouts: 0.01 us -> 2.14 us
    broadcast_in_dim x3 -> x0, local copies, waits for them, and re-layouts: 1.98 us -> none  [the longest x1 0.7 us: per_device(): ax = jnp.broadcast_to(along(offsets[:, 0])[:, :, None], (2, grid, LANES))]
    another operation x3 -> x0, other arithmetic: 1.72 us -> none  [the longest x1 0.97 us: per_device(): result = jnp.stack([total[:, :grid], total[:, HALF:HALF + grid]])]
where the time goes in v1:
time: 66.9 us; the launch traced here: 66.7 us
  Pallas kernels  64.6 us (97%)
  local copies, waits for them, and re-layouts  2.14 us (3%)
    pallas_call x1, Pallas kernels, per_device(): pl.pallas_call(functools.partial(kernel, grid, ring, pools, pitch, BATCH)...  64.6 us
    unnamed x1, local copies, waits for them, and re-layouts  2.14 us

profile of v1, /device:TPU:0, one launch (start us, length us, event | category | flops | bytes accessed | tf_op | source)
XLA Modules:
  0.0 66.7 jit_solution(18415776963816272802)
XLA Ops:
  0.0 64.6 %shard_map.46 = f32[2,48,2304]{2,1,0:T(8,128)} custom-call(s32[8]{0:T(128)} %label_ref.1, bf16[2,48,2304]{2,1,0:T(8,128)(2,1)} %bitcast.5, bf16[2,256,256]{2,1,0:T(8,128)(2,1)} %constant.4.clone.lanes_ref, bf16[96,144]{1,0:T(8,128)(2,1)} %constant.5.clone.rows_ref), custom_call_target="tpu_custom_call" | custom-call | tf_op jit(solution)/shard_map/pallas_call | solution.py:331
  64.6 2.1 %copy.7 = f32[1,2,1,48,2304]{4,3,2,1,0:T(8,128)} copy(f32[1,2,1,48,2304]{4,3,2,1,0:T(8,128)} %bitcast.4) | data formatting | bytes 1769472

commit v2 on v1

--- a/solution.py
+++ b/solution.py
@@ -96,12 +96,12 @@
     def place(plane, band, outer):
         return 2 * visits(ring, plane).index(band) + outer
 
-    def copy(source, step, pool, band, slot):
+    def copy(half, source, step, pool, band, slot):
         return pltpu.make_async_remote_copy(
-            src_ref=source,
-            dst_ref=bufs.at[step],
-            send_sem=send_sem.at[slot],
-            recv_sem=recv_sem.at[step],
+            src_ref=source.at[half],
+            dst_ref=bufs.at[step, half],
+            send_sem=send_sem.at[slot, half],
+            recv_sem=recv_sem.at[step, half],
             device_id=(pool, band),
             device_id_type=MESH,
         )
@@ -128,34 +128,40 @@
             later[step] = copies
         return first, later
 
-    def arrival(step):
-        spot = bufs.at[step]
-        pltpu.make_async_copy(spot, spot, recv_sem.at[step]).wait()
-
-    def service(step, moment):
+    def arrival(step, half):
+        spot = bufs.at[step, half]
+        pltpu.make_async_copy(spot, spot, recv_sem.at[step, half]).wait()
+
+    def moments(distance):
+        if distance == 1:
+            return (2, 2)
+        return (4 * distance - 3, 4 * distance - 2)
+
+    def service(moment, odd_moments):
         for plane in range(ring):
-            order = visits(ring, plane)
-            due = []
-            for at, band in enumerate(order):
-                if at == 0:
-                    continue
-                when = 1 if abs(band - plane) == 1 else 2 * at - 1
-                due.append((when, 2 * at))
+            due = {}
+            for at, band in enumerate(visits(ring, plane)):
+                if at > 0:
+                    for half, when in enumerate(moments(abs(band - plane))):
+                        if when % 2 == odd_moments:
+                            due.setdefault(when, []).append((2 * at, half))
 
             @pl.when(n == plane)
             def _():
-                for when, number in due:
+                for when, events in due.items():
                     @pl.when(moment == when)
                     def _():
-                        arrival(number)
-                        for c in sends(plane)[1][number]:
-                            copy(*c).start()
+                        for number, half in sorted(events, key=lambda e: e[1]):
+                            arrival(number, half)
+                            for c in sends(plane)[1][number]:
+                                copy(half, *c).start()
 
     for plane in range(ring):
         @pl.when(n == plane)
         def _():
             for c in sends(plane)[0]:
-                copy(*c).start()
+                for half in range(2):
+                    copy(half, *c).start()
 
     lane = lax.broadcasted_iota(jnp.int32, (1, LANES), 1)
     sign = jnp.where(lane < HALF, 1.0, -1.0).astype(jnp.float32)
@@ -225,11 +231,12 @@
     def one_field(step, carry):
         @pl.when(step % 2 == 1)
         def _():
-            service(step, step)
+            service(2 * step, 0)
 
         @pl.when(jnp.logical_or(step == 0, step % 2 == 1))
         def _():
-            arrival(step)
+            for half in range(2):
+                arrival(step, half)
 
         which = step % 2
         source = bufs.at[step]
@@ -245,6 +252,10 @@
             outs = along_rows([spec[j * grid : (j + 1) * grid] for j in range(batch)], 1)
             for j in range(batch):
                 field[(base + j) * pitch : (base + j) * pitch + grid, :] = outs[j]
+
+        @pl.when(step % 2 == 0)
+        def _():
+            service(2 * step + 1, 1)
 
         for base in range(0, grid, batch):
             xs = [field[pl.ds(base + j, grid, stride=pitch), :] for j in range(batch)]
@@ -285,8 +296,6 @@
     acc2[...] = jnp.zeros_like(acc2)
     lax.fori_loop(0, 2 * ring, one_field, 0)
 
-    weight = -((2.0 * ROUNDS * ring) ** (-0.5))
-
     def finish(g, carry):
         made = [[None] * (group // LANES) for _ in range(2)]
         for j in range(lines):
@@ -296,7 +305,7 @@
             start = j * grid
             at, off = start // LANES, start % LANES
             for part, value in enumerate((one - swap(one), two + swap(two))):
-                value = pltpu.roll(value * weight, off, 1) if off else value * weight
+                value = pltpu.roll(value, off, 1) if off else value
                 row = made[part]
                 row[at] = value if off == 0 else jnp.where(lane < off, row[at], value)
                 if off + grid > LANES:
@@ -313,15 +322,14 @@
         @pl.when(n == plane)
         def _():
             begun, later = sends(plane)
-            for c in begun:
-                copy(*c).wait_send()
-            for copies in later.values():
+            for copies in [begun, *later.values()]:
                 for c in copies:
-                    copy(*c).wait_send()
+                    for half in range(2):
+                        copy(half, *c).wait_send()
 
 
 def per_device(psi, kpoint_of_pool):
-    own = psi[0, :, 0]
+    own, own_bands = psi[0, :, 0], psi.shape[2]
     grid, points = own.shape[1], own.shape[2]
     ring = lax.axis_size("band")
     pools = lax.axis_size("kpool")
@@ -342,12 +350,13 @@
             pltpu.VMEM((points, LANES), jnp.float32),
             pltpu.VMEM((points, LANES), jnp.float32),
             pltpu.VMEM((2, grid, grid, LANES), jnp.float32),
-            pltpu.SemaphoreType.DMA((2 * ring,)),
-            pltpu.SemaphoreType.DMA((4 + 2 * ring,)),
+            pltpu.SemaphoreType.DMA((2 * ring, 2)),
+            pltpu.SemaphoreType.DMA((4 + 2 * ring, 2)),
         ],
         compiler_params=pltpu.CompilerParams(collective_id=0, has_side_effects=True),
     )(kpoint_of_pool, own, jnp.asarray(lanes), jnp.asarray(rows))
-    return total[None, :, None]
+    weight = -((2.0 * ROUNDS * ring * own_bands) ** (-0.5))
+    return (total * weight)[None, :, None]
 
 
 def solution(mesh):

time: 66.9 us -> 64.5 us (0.964)
  the two profiles are of different devices: /device:TPU:0 before, /device:TPU:16 now
where the time goes in v2:
time: 64.5 us; the launch traced here: 64.4 us
  Pallas kernels  62.2 us (96%)
  other arithmetic  2.16 us (3%)
    pallas_call x1, Pallas kernels, per_device(): pl.pallas_call(functools.partial(kernel, grid, ring, pools, pitch, BATCH)...  62.2 us
    broadcast_in_dim x1, other arithmetic, per_device(): return (total * weight)[None, :, None]  2.16 us

profile of v2, /device:TPU:16, one launch (start us, length us, event | category | flops | bytes accessed | tf_op | source)
XLA Modules:
  0.0 64.4 jit_solution(16365131553482923701)
XLA Ops:
  0.0 62.2 %shard_map.46 = f32[2,48,2304]{2,1,0:T(8,128)} custom-call(s32[8]{0:T(128)} %label_ref.1, bf16[2,48,2304]{2,1,0:T(8,128)(2,1)} %bitcast.5, bf16[2,256,256]{2,1,0:T(8,128)(2,1)} %constant.6.clone.lanes_ref, bf16[96,144]{1,0:T(8,128)(2,1)} %constant.7.clone.rows_ref), custom_call_target="tpu_custom_call" | custom-call | tf_op jit(solution)/shard_map/pallas_call | solution.py:339
  62.2 2.2 %multiply_bitcast_fusion = f32[1,2,1,48,2304]{4,3,2,1,0:T(8,128)} fusion(f32[2,48,2304]{2,1,0:T(8,128)} %shard_map.46), kind=kLoop, calls=%fused_computation | loop fusion | flops 221184 | bytes 1769472 | tf_op jit(solution)/shard_map/broadcast_in_dim | solution.py:359

commit v3 on v2

--- a/solution.py
+++ b/solution.py
@@ -55,8 +55,64 @@
     return high, low
 
 
-def visits(ring, n):
-    return [n] + sorted((m for m in range(ring) if m != n), key=lambda m: (abs(m - n), (m - n) % 2 * 0 + (m ^ 1 != n)))
+def over_z(ring, plane, band, parity):
+    if 0 < plane < ring - 1:
+        return abs(band - plane) == 1
+    return parity == 0 and abs(band - plane) == ring - 1 > 1
+
+
+def visits(ring, plane):
+    inner = 0 < plane < ring - 1
+    others = sorted((m for m in range(ring) if m != plane), key=lambda m: (abs(m - plane), m ^ 1 != plane))
+    order = [(0, plane), (1, plane)]
+    if not inner:
+        for band in others:
+            order += [(0, band), (1, band)]
+        return order
+    close = [m for m in others if abs(m - plane) == 1]
+    distant = [m for m in others if abs(m - plane) > 1]
+    order += [(0, m) for m in close] + [(1, close[0])]
+    for band in distant:
+        order += [(0, band), (1, band)]
+    return order + [(1, m) for m in close[1:]]
+
+
+def forwards(ring, plane, parity, kind, band):
+    found = []
+    if kind == 0 and band != plane:
+        onward = plane + 1 if band < plane else plane - 1
+        if 0 <= onward < ring:
+            found.append((0, "me", onward))
+        if not over_z(ring, plane, band, parity):
+            found.append((1, "beyond", plane))
+    if kind == 1:
+        for onward in (plane - 1, plane + 1):
+            if 0 <= onward < ring and (band - plane) * (plane - onward) >= 0:
+                if over_z(ring, onward, band, parity):
+                    found.append((1, "me", onward))
+    return found
+
+
+def moments(ring, plane, parity):
+    inner = 0 < plane < ring - 1
+    table = {}
+    for step, (kind, band) in enumerate(visits(ring, plane)):
+        distance = abs(band - plane)
+        when = (2 * step, 2 * step)
+        sends = forwards(ring, plane, parity, kind, band)
+        if sends and kind == 0:
+            if distance == 1:
+                when = (1, 2)
+            elif distance == 2:
+                when = (5, 7) if inner else (5, 6)
+            else:
+                when = (4 * distance - 3, 4 * distance - 2)
+        elif sends and distance > 0:
+            when = (2 * step - 3, 2 * step - 1)
+        for half in range(2):
+            assert when[half] <= 2 * step
+            table.setdefault(when[half], []).append((kind, half, step, sends, band))
+    return {when: sorted(events, key=lambda e: e[:3]) for when, events in table.items()}
 
 
 def squares(offset, grid, index):
@@ -93,8 +149,8 @@
                     count += 2
             pl.semaphore_wait(barrier, count)
 
-    def place(plane, band, outer):
-        return 2 * visits(ring, plane).index(band) + outer
+    def place(plane, band, kind):
+        return visits(ring, plane).index((kind, band))
 
     def copy(half, source, step, pool, band, slot):
         return pltpu.make_async_remote_copy(
@@ -106,62 +162,57 @@
             device_id_type=MESH,
         )
 
-    def sends(plane):
-        first = [(sent_ref, place(plane, plane, 0), near, plane, 0)]
-        first.append((sent_ref, place(plane, plane, 1), far, plane, 1))
-        slot = 2
+    def own_sends(plane):
+        found = [
+            (sent_ref, place(plane, plane, 0), near, plane, 0),
+            (sent_ref, place(plane, plane, 1), far, plane, 1),
+        ]
         for other in (plane - 1, plane + 1):
             if 0 <= other < ring:
-                first.append((sent_ref, place(other, plane, 0), near, other, slot))
+                found.append((sent_ref, place(other, plane, 0), near, other, len(found)))
+        return found
+
+    def later_sends(plane, parity):
+        found, slot = {}, 4
+        for step, (kind, band) in enumerate(visits(ring, plane)):
+            found[step] = []
+            for to_kind, pool, onward in forwards(ring, plane, parity, kind, band):
+                target = me if pool == "me" else beyond
+                found[step].append((bufs.at[step], place(onward, band, to_kind), target, onward, slot))
                 slot += 1
-        later = {}
-        for band in visits(ring, plane)[1:]:
-            step = place(plane, band, 0)
-            source = bufs.at[step]
-            onward = plane + 1 if band < plane else plane - 1
-            copies = []
-            if 0 <= onward < ring:
-                copies.append((source, place(onward, band, 0), me, onward, slot))
-                slot += 1
-            copies.append((source, place(plane, band, 1), beyond, plane, slot))
-            slot += 1
-            later[step] = copies
-        return first, later
-
-    def arrival(step, half):
-        spot = bufs.at[step, half]
-        pltpu.make_async_copy(spot, spot, recv_sem.at[step, half]).wait()
-
-    def moments(distance):
-        if distance == 1:
-            return (2, 2)
-        return (4 * distance - 3, 4 * distance - 2)
-
-    def service(moment, odd_moments):
+        return found
+
+    def classes(act):
         for plane in range(ring):
-            due = {}
-            for at, band in enumerate(visits(ring, plane)):
-                if at > 0:
-                    for half, when in enumerate(moments(abs(band - plane))):
-                        if when % 2 == odd_moments:
-                            due.setdefault(when, []).append((2 * at, half))
-
-            @pl.when(n == plane)
-            def _():
-                for when, events in due.items():
-                    @pl.when(moment == when)
+            for parity in range(2):
+                pl.when(jnp.logical_and(n == plane, odd == parity))(functools.partial(act, plane, parity))
+
+    def service(step, middle):
+        def act(plane, parity):
+            for when, events in moments(ring, plane, parity).items():
+                if when % 2 == middle:
+
+                    @pl.when(step == when // 2)
                     def _():
-                        for number, half in sorted(events, key=lambda e: e[1]):
-                            arrival(number, half)
-                            for c in sends(plane)[1][number]:
+                        for kind, half, number, sends, band in events:
+                            spot = bufs.at[number, half]
+                            pltpu.make_async_copy(spot, spot, recv_sem.at[number, half]).wait()
+                            for c in later_sends(plane, parity)[number]:
                                 copy(half, *c).start()
 
+        classes(act)
+
+    def begin(plane, parity):
+        for c in own_sends(plane):
+            for half in range(2):
+                copy(half, *c).start()
+
+    classes(begin)
+
+    lists = 0
     for plane in range(ring):
-        @pl.when(n == plane)
-        def _():
-            for c in sends(plane)[0]:
-                for half in range(2):
-                    copy(half, *c).start()
+        bits = sum(kind << step for step, (kind, _) in enumerate(visits(ring, plane)))
+        lists = lists + (n == plane).astype(jnp.int32) * bits
 
     lane = lax.broadcasted_iota(jnp.int32, (1, LANES), 1)
     sign = jnp.where(lane < HALF, 1.0, -1.0).astype(jnp.float32)
@@ -229,16 +280,8 @@
         return outs
 
     def one_field(step, carry):
-        @pl.when(step % 2 == 1)
-        def _():
-            service(2 * step, 0)
-
-        @pl.when(jnp.logical_or(step == 0, step % 2 == 1))
-        def _():
-            for half in range(2):
-                arrival(step, half)
-
-        which = step % 2
+        service(step, 0)
+        which = jnp.right_shift(lists, step) % 2
         source = bufs.at[step]
 
         for base in range(0, grid, batch):
@@ -253,9 +296,7 @@
             for j in range(batch):
                 field[(base + j) * pitch : (base + j) * pitch + grid, :] = outs[j]
 
-        @pl.when(step % 2 == 0)
-        def _():
-            service(2 * step + 1, 1)
+        service(step, 1)
 
         for base in range(0, grid, batch):
             xs = [field[pl.ds(base + j, grid, stride=pitch), :] for j in range(batch)]
@@ -318,14 +359,13 @@
 
     lax.fori_loop(0, grid // lines, finish, 0)
 
-    for plane in range(ring):
-        @pl.when(n == plane)
-        def _():
-            begun, later = sends(plane)
-            for copies in [begun, *later.values()]:
-                for c in copies:
-                    for half in range(2):
-                        copy(half, *c).wait_send()
+    def settle(plane, parity):
+        for copies in [own_sends(plane), *later_sends(plane, parity).values()]:
+            for c in copies:
+                for half in range(2):
+                    copy(half, *c).wait_send()
+
+    classes(settle)
 
 
 def per_device(psi, kpoint_of_pool):
@@ -340,7 +380,7 @@
         functools.partial(kernel, grid, ring, pools, pitch, BATCH),
         in_specs=[pl.BlockSpec(memory_space=pltpu.SMEM)] + [whole] * 3,
         out_specs=whole,
-        out_shape=jax.ShapeDtypeStruct(own.shape, jnp.float32),
+        out_shape=pltpu.VMEM(own.shape, jnp.float32),
         scratch_shapes=[
             pltpu.VMEM((2 * ring,) + own.shape, jnp.bfloat16),
             pltpu.VMEM((grid * pitch, LANES), jnp.float32),
@@ -351,7 +391,7 @@
             pltpu.VMEM((points, LANES), jnp.float32),
             pltpu.VMEM((2, grid, grid, LANES), jnp.float32),
             pltpu.SemaphoreType.DMA((2 * ring, 2)),
-            pltpu.SemaphoreType.DMA((4 + 2 * ring, 2)),
+            pltpu.SemaphoreType.DMA((4 + 3 * ring, 2)),
         ],
         compiler_params=pltpu.CompilerParams(collective_id=0, has_side_effects=True),
     )(kpoint_of_pool, own, jnp.asarray(lanes), jnp.asarray(rows))

time: 64.5 us -> 63.8 us (0.989)
  the two profiles are of different devices: /device:TPU:16 before, /device:TPU:0 now
where the time goes in v3:
time: 63.8 us; the launch traced here: 63.3 us
  Pallas kernels  62.3 us (98%)
  other arithmetic  0.99 us (2%)
    pallas_call x1, Pallas kernels, per_device(): pl.pallas_call(functools.partial(kernel, grid, ring, pools, pitch, BATCH)...  62.3 us

profile of v3, /device:TPU:0, one launch (start us, length us, event | category | flops | bytes accessed | tf_op | source)
XLA Modules:
  0.0 63.3 jit_solution(11692812541995718930)
XLA Ops:
  0.0 62.3 %shard_map.46 = f32[2,48,2304]{2,1,0:T(8,128)S(1)} custom-call(s32[8]{0:T(128)} %label_ref.1, bf16[2,48,2304]{2,1,0:T(8,128)(2,1)} %bitcast.5, bf16[2,256,256]{2,1,0:T(8,128)(2,1)} %constant.6.clone.lanes_ref, bf16[96,144]{1,0:T(8,128)(2,1)} %constant.7.clone.rows_ref), custom_call_target="tpu_custom_call" | custom-call | tf_op jit(solution)/shard_map/pallas_call | solution.py:379
  62.3 1.0 %multiply_bitcast_fusion = f32[1,2,1,48,2304]{4,3,2,1,0:T(8,128)} fusion(f32[2,48,2304]{2,1,0:T(8,128)S(1)} %shard_map.46), kind=kLoop, calls=%fused_computation | loop fusion | flops 221184 | bytes 1769472 | tf_op jit(solution)/shard_map/broadcast_in_dim | solution.py:399

commit v4 on v3

--- a/solution.py
+++ b/solution.py
@@ -109,6 +109,7 @@
                 when = (4 * distance - 3, 4 * distance - 2)
         elif sends and distance > 0:
             when = (2 * step - 3, 2 * step - 1)
+        when = tuple(min(w + w % 2, 2 * step) for w in when)
         for half in range(2):
             assert when[half] <= 2 * step
             table.setdefault(when[half], []).append((kind, half, step, sends, band))

time: 63.8 us -> 51.3 us (0.80)
  Pallas kernels: 62.3 us -> 49.3 us
    pallas_call x1, Pallas kernels: 62.3 us -> 49.3 us  [per_device(): pl.pallas_call(functools.partial(kernel, grid, ring, pools, pitch, BATCH)...]
where the time goes in v4:
time: 51.3 us; the launch traced here: 50.3 us
  Pallas kernels  49.3 us (96%)
  other arithmetic  0.99 us (2%)
    pallas_call x1, Pallas kernels, per_device(): pl.pallas_call(functools.partial(kernel, grid, ring, pools, pitch, BATCH)...  49.3 us

profile of v4, /device:TPU:0, one launch (start us, length us, event | category | flops | bytes accessed | tf_op | source)
XLA Modules:
  0.0 50.3 jit_solution(14369036503351909722)
XLA Ops:
  0.0 49.3 %shard_map.46 = f32[2,48,2304]{2,1,0:T(8,128)S(1)} custom-call(s32[8]{0:T(128)} %label_ref.1, bf16[2,48,2304]{2,1,0:T(8,128)(2,1)} %bitcast.5, bf16[2,256,256]{2,1,0:T(8,128)(2,1)} %constant.6.clone.lanes_ref, bf16[96,144]{1,0:T(8,128)(2,1)} %constant.7.clone.rows_ref), custom_call_target="tpu_custom_call" | custom-call | tf_op jit(solution)/shard_map/pallas_call | solution.py:380
  49.4 1.0 %multiply_bitcast_fusion = f32[1,2,1,48,2304]{4,3,2,1,0:T(8,128)} fusion(f32[2,48,2304]{2,1,0:T(8,128)S(1)} %shard_map.46), kind=kLoop, calls=%fused_computation | loop fusion | flops 221184 | bytes 1769472 | tf_op jit(solution)/shard_map/broadcast_in_dim | solution.py:400
